TPU v7x, 32 devices: a whole 2x2x4 slice. The times are simulated.
32 devices in a mesh: blk: 8 (over y, x, core), chan: 4 (over z).
Axes of the slice: x: 2, y: 2, z: 4, core: 2. Of those that a mesh axis runs over, the one named last changes fastest.
Arguments:
- positions: float32 [3, 1024], P(None, 'blk'), may hold values from 0 to 48, as said below
- species: int32 [1024], P('blk'), may hold values from 0 to 1
- node_features: float32 [64, 1024], P('chan', 'blk'), may hold values from -6 to 6
- block_mask: int32 [8, 7], P('blk'), may hold values from 0 to 1, as said below
- radial_weight: float32 [8, 64], P(None, 'chan'), may hold values from -2 to 2
- species_embed: float32 [64, 2], P('chan'), may hold values from 0.25 to 1.75
- center_embed: float32 [64, 2], P('chan'), may hold values from 0.25 to 1.75
- mix_weight: float32 [3, 64, 64], replicated, may hold values from -0.75 to 0.75
Outputs:
- descriptors: float32 [3, 64, 1024], P(None, 'chan', 'blk')
Inputs may be any that keep to these rules, and one draw needn't show every extreme that they name: `positions`: atom g lies in slab s = g // 128: its first coordinate in [s * 5 / 3, (s + 1) * 5 / 3), the other two in [0, 48). An arbitrary set of kept slab pairs, symmetric between the two slabs of a pair: block_mask[i, 3 + k] equals block_mask[(i + k) mod 8, 3 - k]; the middle column is 1.
All inputs are finite; a program needn't handle non-finite values.
Results may differ from a plain program's by a relative error of at most 0.0035.
Values sent between devices are 32-bit elements; how exact they have to be, the bound alone decides.
No kernel may reach another device: no remote copies, remote signals or barrier semaphores. Data moves between devices by JAX's collectives and lax.ppermute only.
A program may use at most 64 MiB of HBM per device.

v0:
```python
import math
import jax
import jax.numpy as jnp
from jax import lax
from jax.sharding import PartitionSpec as P

slab_width = 5.0 / 3.0
cross_width = 48.0
cut_radius = 5.0
soften = 0.25


def from_behind(value, axis, by):
    size = lax.axis_size(axis)
    return lax.ppermute(value, axis, [(i, (i + by) % size) for i in range(size)])


def table_of(own_pos, other_pos, box_x, keep_pairs, count):
    separation = other_pos[:, None, :] - own_pos[:, :, None]
    lengths = jnp.array([box_x, cross_width, cross_width], dtype=jnp.float32)[:, None, None]
    separation = separation - lengths * jnp.floor(separation / lengths + 0.5)
    distance = jnp.sqrt(jnp.sum(separation * separation, axis=0) + soften)
    unit_x = separation[0] / distance
    unit_y = separation[1] / distance
    unit_z = separation[2] / distance
    root3 = math.sqrt(3.0)
    root15 = math.sqrt(15.0)
    harmonics = jnp.stack(
        [
            jnp.ones_like(distance),
            root3 * unit_x,
            root3 * unit_y,
            root3 * unit_z,
            root15 * unit_x * unit_y,
            root15 * unit_y * unit_z,
            0.5 * math.sqrt(5.0) * (2.0 * unit_z * unit_z - unit_x * unit_x - unit_y * unit_y),
            root15 * unit_x * unit_z,
            0.5 * root15 * (unit_x * unit_x - unit_y * unit_y),
        ]
    )
    scaled = distance / cut_radius
    polynomial = 1.0 - 28.0 * scaled**6 + 48.0 * scaled**7 - 21.0 * scaled**8
    envelope = jnp.where(scaled < 1.0, polynomial, 0.0) * keep_pairs
    orders = jnp.arange(1, count + 1, dtype=jnp.float32)[:, None, None]
    radial = (
        math.sqrt(2.0 / cut_radius)
        * jnp.sin(orders * (math.pi / cut_radius) * distance[None])
        / distance[None]
        * envelope[None]
    )
    return (radial[:, None] * harmonics[None]).astype(jnp.bfloat16)


def weights_lm(mix_weight):
    return jnp.concatenate(
        [
            mix_weight[0:1],
            jnp.repeat(mix_weight[1:2], 3, axis=0),
            jnp.repeat(mix_weight[2:3], 5, axis=0),
        ],
        axis=0,
    )


def describe(mixed_tensor):
    squares = mixed_tensor * mixed_tensor
    return jnp.log1p(
        jnp.stack(
            [squares[:, 0], jnp.sum(squares[:, 1:4], axis=1), jnp.sum(squares[:, 4:9], axis=1)]
        )
    )


def one_hot_of(species, kinds):
    return (species[None, :] == jnp.arange(kinds, dtype=jnp.int32)[:, None]).astype(jnp.float32)


def carried_of(species, node_features, species_embed, radial_weight):
    embedded = jnp.dot(
        species_embed, one_hot_of(species, species_embed.shape[1]), precision=lax.Precision.HIGHEST
    )
    return (radial_weight[:, :, None] * (node_features * embedded)[None]).astype(jnp.bfloat16)


def contributions(own_pos, other_pos, other_carried, active, box_x, count):
    forward_shape = (other_carried.shape[1], 9, own_pos.shape[1])

    def compute():
        pair_table = table_of(own_pos, other_pos, box_x, active.astype(jnp.float32), count)
        forward = jnp.einsum(
            "ncb,nmab->cma", other_carried, pair_table, preferred_element_type=jnp.float32
        )
        return forward

    def skipped():
        return jnp.zeros(forward_shape, jnp.float32)

    return lax.cond(active > 0, compute, skipped)


def step_ahead(bundle):
    return from_behind(bundle, "blk", -1)


def shards(
    positions,
    species,
    node_features,
    block_mask,
    radial_weight,
    species_embed,
    center_embed,
    mix_weight,
):
    box_x = float(lax.axis_size("blk")) * slab_width
    reach = (block_mask.shape[1] - 1) // 2
    count = radial_weight.shape[0]
    atom_count = positions.shape[1]
    feats_all, spec_all, cent_all, radial_all = (
        node_features,
        species_embed,
        center_embed,
        radial_weight,
    )
    centre_rows = jnp.arange(atom_count, dtype=jnp.int32)
    no_self = 1.0 - (
        centre_rows[:, None] == jnp.arange(atom_count, dtype=jnp.int32)[None, :]
    ).astype(jnp.float32)
    slab_carried = carried_of(species, feats_all, spec_all, radial_all)
    self_table = table_of(
        positions, positions, box_x, block_mask[0, reach].astype(jnp.float32) * no_self, count
    )
    summed = jnp.einsum(
        "ncb,nmab->cma", slab_carried, self_table, preferred_element_type=jnp.float32
    )
    ahead = (positions, species, feats_all)
    behind = ahead
    for offset in range(1, reach + 1):
        ahead = step_ahead(ahead)
        ahead_carried = carried_of(ahead[1], ahead[2], spec_all, radial_all)
        summed = summed + contributions(
            positions, ahead[0], ahead_carried, block_mask[0, reach + offset], box_x, count
        )
        behind = from_behind((behind[0], behind[1], behind[2]), "blk", 1)
        behind_carried = carried_of(behind[1], behind[2], spec_all, radial_all)
        summed = summed + contributions(
            positions, behind[0], behind_carried, block_mask[0, reach - offset], box_x, count
        )
    centre = jnp.dot(
        cent_all, one_hot_of(species, cent_all.shape[1]), precision=lax.Precision.HIGHEST
    )
    features = summed * centre[:, None, :]
    weights_all = weights_lm(mix_weight)
    channel_count = features.shape[0]
    weights_out = lax.dynamic_slice_in_dim(
        weights_all, lax.axis_index("chan") * channel_count, channel_count, 1
    )
    mixed_tensor = jnp.einsum(
        "mpc,cma->pma",
        weights_out,
        lax.all_gather(features, "chan", axis=0, tiled=True),
        precision=lax.Precision.HIGHEST,
    )
    return describe(mixed_tensor)


def solution(mesh):
    return jax.shard_map(
        shards,
        mesh=mesh,
        in_specs=(
            P(None, "blk"),
            P("blk"),
            P("chan", "blk"),
            P("blk", None),
            P(None, "chan"),
            P("chan", None),
            P("chan", None),
            P(),
        ),
        out_specs=P(None, "chan", "blk"),
        check_vma=False,
    )
```

profile of v0, /device:TPU:0, one launch (start us, length us, event | category | flops | bytes accessed | tf_op | source)
XLA Modules:
  0.0 70.0 jit_solution(16418820313768697507)
XLA Ops:
  0.5 2.9 %collective-permute-start.2 = (s32[128]{0:T(128)}, s32[128]{0:T(128)S(1)}, u32[]{:S(2)}, u32[]{:S(2)}) collective-permute-start(s32[128]{0:T(128)} %param.28), channel_id=1, source_target_pairs={{0,28},{4,0},{8,4},{12,8},{16,12},{20,16},{24,20},{28,24},{1,29},{... | collective-permute-start | bytes 1544 | tf_op jit(solution)/shard_map/ppermute | solution.py:15
  4.1 0.8 %collective-permute-start.4 = (f32[16,128]{1,0:T(8,128)}, f32[16,128]{1,0:T(8,128)S(1)}, u32[]{:S(2)}, u32[]{:S(2)}) collective-permute-start(f32[16,128]{1,0:T(8,128)} %param.29), channel_id=1, source_target_pairs={{0,4},{4,8},{8,12},{12,16},{16,20},{20,24},{24,28},{28,0},{1,5},{5... | collective-permute-start | bytes 24584 | tf_op jit(solution)/shard_map/ppermute | solution.py:15
  4.9 0.9 %multiply_reduce_fusion.6 = (f32[128,128]{1,0:T(8,128)S(1)}, f32[3,128,128]{2,1,0:T(8,128)S(1)}) fusion(f32[3]{0:T(128)} %constant.184, f32[3]{0:T(128)} %constant.182.clone, f32[3,128]{1,0:T(4,128)} %param.27), kind=kLoop, calls=%fused_computation.331 | loop fusion | flops 376832 | bytes 263704 | tf_op jit(solution)/shard_map/reduce_sum | solution.py:22
  8.5 1.8 %divide_multiply_fusion.6 = f32[8,128,128]{2,1,0:T(8,128)S(1)} fusion(f32[128,128]{1,0:T(8,128)S(1)} %get-tuple-element.162, f32[128,128]{1,0:T(8,128)S(1)} %get-tuple-element.161, f32[8]{0:T(128)S(1)} %add_multiply_fusion.7), kind=kLoop, calls=%fused_computation.322 | loop fusion | flops 524288 | bytes 655392 | tf_op jit(solution)/shard_map/mul | solution.py:46
  10.3 0.7 %fusion.159 = f32[16,9,128]{2,0,1:T(8,128)S(1)} fusion(f32[9,128,128]{2,1,0:T(8,128)S(1)} %multiply_dynamic-update-slice_fusion.24, f32[8,128,128]{2,1,0:T(8,128)S(1)} %divide_multiply_fusion.6, f32[16,128]{1,0:T(8,128)S(1)} %fusion.167, f32[8,16]{1,0:T(8,128)S(1)} %copy-done.5), kind=kOutput, calls=%fused_computation.305 | convolution fusion | flops 40140800 | bytes 1196544 | tf_op jit(solution)/shard_map/ncb,nmab->cma/dot_general | solution.py:133
  13.0 1.9 %collective-permute-start.6 = (f32[3,128]{1,0:T(4,128)S(1)}, f32[3,128]{1,0:T(4,128)S(1)}, u32[]{:S(2)}, u32[]{:S(2)}) collective-permute-start(f32[3,128]{1,0:T(4,128)S(1)} %collective-permute-done), channel_id=1, source_target_pairs={{0,28},{4,0},{8,4},{12,8},{16,12},{20,16},{24,20},{28,24},{1,29},{... | collective-permute-start | bytes 4616 | tf_op jit(solution)/shard_map/ppermute | solution.py:15
  16.8 0.7 %collective-permute-start.11 = (s32[128]{0:T(128)S(1)}, s32[128]{0:T(128)S(1)}, u32[]{:S(2)}, u32[]{:S(2)}) collective-permute-start(s32[128]{0:T(128)S(1)} %collective-permute-done.5), channel_id=1, source_target_pairs={{0,4},{4,8},{8,12},{12,16},{16,20},{20,24},{24,28},{28,0},{1,5},{5... | collective-permute-start | bytes 1544 | tf_op jit(solution)/shard_map/ppermute | solution.py:15
  17.6 2.0 %collective-permute-start.8 = (s32[128]{0:T(128)S(1)}, s32[128]{0:T(128)S(1)}, u32[]{:S(2)}, u32[]{:S(2)}) collective-permute-start(s32[128]{0:T(128)S(1)} %collective-permute-done.2), channel_id=1, source_target_pairs={{0,28},{4,0},{8,4},{12,8},{16,12},{20,16},{24,20},{28,24},{1,29},{... | collective-permute-start | bytes 1544 | tf_op jit(solution)/shard_map/ppermute | solution.py:15
  19.6 1.2 %collective-permute-done.11 = s32[128]{0:T(128)S(1)} collective-permute-done((s32[128]{0:T(128)S(1)}, s32[128]{0:T(128)S(1)}, u32[]{:S(2)}, u32[]{:S(2)}) %collective-permute-start.11) | collective-permute-done | bytes 544 | tf_op jit(solution)/shard_map/ppermute | solution.py:15
  20.9 1.0 %collective-permute-start.17 = (s32[128]{0:T(128)S(1)}, s32[128]{0:T(128)S(1)}, u32[]{:S(2)}, u32[]{:S(2)}) collective-permute-start(s32[128]{0:T(128)S(1)} %collective-permute-done.11), channel_id=1, source_target_pairs={{0,4},{4,8},{8,12},{12,16},{16,20},{20,24},{24,28},{28,0},{1,5},{5... | collective-permute-start | bytes 1544 | tf_op jit(solution)/shard_map/ppermute | solution.py:15
  21.9 1.7 %collective-permute-start.14 = (s32[128]{0:T(128)S(1)}, s32[128]{0:T(128)S(1)}, u32[]{:S(2)}, u32[]{:S(2)}) collective-permute-start(s32[128]{0:T(128)S(1)} %collective-permute-done.8), channel_id=1, source_target_pairs={{0,28},{4,0},{8,4},{12,8},{16,12},{20,16},{24,20},{28,24},{1,29},{... | collective-permute-start | bytes 1544 | tf_op jit(solution)/shard_map/ppermute | solution.py:15
  25.1 3.1 %collective-permute-done.10 = f32[16,128]{1,0:T(8,128)S(1)} collective-permute-done((f32[16,128]{1,0:T(8,128)S(1)}, f32[16,128]{1,0:T(8,128)S(1)}, u32[]{:S(2)}, u32[]{:S(2)}) %collective-permute-start.10) | collective-permute-done | bytes 8224 | tf_op jit(solution)/shard_map/ppermute | solution.py:15
  28.4 1.2 %collective-permute-done.7 = f32[16,128]{1,0:T(8,128)S(1)} collective-permute-done((f32[16,128]{1,0:T(8,128)S(1)}, f32[16,128]{1,0:T(8,128)S(1)}, u32[]{:S(2)}, u32[]{:S(2)}) %collective-permute-start.7) | collective-permute-done | bytes 8224 | tf_op jit(solution)/shard_map/ppermute | solution.py:15
  30.3 2.2 %collective-permute-start.13 = (f32[16,128]{1,0:T(8,128)S(1)}, f32[16,128]{1,0:T(8,128)S(1)}, u32[]{:S(2)}, u32[]{:S(2)}) collective-permute-start(f32[16,128]{1,0:T(8,128)S(1)} %collective-permute-done.7), channel_id=1, source_target_pairs={{0,28},{4,0},{8,4},{12,8},{16,12},{20,16},{24,20},{28,24},{1,29},{... | collective-permute-start | bytes 24584 | tf_op jit(solution)/shard_map/ppermute | solution.py:15
  32.5 1.1 %collective-permute-done.16 = f32[16,128]{1,0:T(8,128)S(1)} collective-permute-done((f32[16,128]{1,0:T(8,128)S(1)}, f32[16,128]{1,0:T(8,128)S(1)}, u32[]{:S(2)}, u32[]{:S(2)}) %collective-permute-start.16) | collective-permute-done | bytes 8224 | tf_op jit(solution)/shard_map/ppermute | solution.py:15
  34.2 3.7 %conditional.8 = (f32[16,9,128]{2,0,1:T(8,128)S(1)}) conditional(s32[]{:T(128)} %convert_element_type.108, () %tuple.45, (f32[3,128]{1,0:T(4,128)S(1)}, f32[3,128]{1,0:T(4,128)S(1)}, f32[3]{0:T(128)S(1)}, s32[]{:T(128)}, bf16[8,16,128]{2,1,0:T(8,128)(2,1)S(1)}) %tuple.113), branch_computations={%region_7.8_spmd, %region_8.10_spmd} | conditional | flops 41861136 | bytes 4435040 | solution.py:98
  35.4 1.8 %divide_multiply_fusion.2 = f32[8,128,128]{2,1,0:T(8,128)S(1)} fusion(f32[128,128]{1,0:T(8,128)S(1)} %get-tuple-element.143, f32[128,128]{1,0:T(8,128)S(1)} %get-tuple-element.142, f32[8]{0:T(128)S(1)} %add_multiply_fusion.2), kind=kLoop, calls=%fused_computation.105 | loop fusion | flops 524288 | bytes 655392 | tf_op jit(solution)/shard_map/cond/branch_1_fun/mul | solution.py:46
  37.2 0.7 %fusion.55 = f32[16,9,128]{2,0,1:T(8,128)S(1)} fusion(f32[9,128,128]{2,1,0:T(8,128)S(1)} %multiply_dynamic-update-slice_fusion.8, f32[8,128,128]{2,1,0:T(8,128)S(1)} %divide_multiply_fusion.2, bf16[8,16,128]{2,1,0:T(8,128)(2,1)S(1)} %get-tuple-element.97), kind=kOutput, calls=%fused_computation.104 | convolution fusion | flops 40108032 | bytes 1220608 | tf_op jit(solution)/shard_map/cond/branch_1_fun/ncb,nmab->cma/dot_general | solution.py:90
  37.9 4.5 %conditional.9 = (f32[16,9,128]{2,0,1:T(8,128)S(1)}) conditional(s32[]{:T(128)} %convert_element_type.110, () %tuple.47, (f32[3,128]{1,0:T(4,128)}, f32[3,128]{1,0:T(4,128)S(1)}, f32[3]{0:T(128)S(1)}, s32[]{:T(128)}, bf16[8,16,128]{2,1,0:T(8,128)(2,1)S(1)}) %tuple.114), branch_computations={%region_10.11_spmd, %region_11.13_spmd} | conditional | flops 41861136 | bytes 4435040 | solution.py:98
  38.0 0.8 %multiply_reduce_fusion.3 = (f32[128,128]{1,0:T(8,128)S(1)}, f32[3,128,128]{2,1,0:T(8,128)S(1)}) fusion(f32[3]{0:T(128)S(1)} %get-tuple-element.100, f32[3,128]{1,0:T(4,128)S(1)} %get-tuple-element.99, f32[3,128]{1,0:T(4,128)} %get-tuple-element.98), kind=kLoop, calls=%fused_computation.161 | loop fusion | flops 376832 | bytes 265228 | tf_op jit(solution)/shard_map/cond/branch_1_fun/reduce_sum | solution.py:22
  39.9 1.8 %divide_multiply_fusion.3 = f32[8,128,128]{2,1,0:T(8,128)S(1)} fusion(f32[128,128]{1,0:T(8,128)S(1)} %get-tuple-element.147, f32[128,128]{1,0:T(8,128)S(1)} %get-tuple-element.146, f32[8]{0:T(128)S(1)} %add_multiply_fusion.3), kind=kLoop, calls=%fused_computation.155 | loop fusion | flops 524288 | bytes 655392 | tf_op jit(solution)/shard_map/cond/branch_1_fun/mul | solution.py:46
  41.7 0.7 %fusion.81 = f32[16,9,128]{2,0,1:T(8,128)S(1)} fusion(f32[9,128,128]{2,1,0:T(8,128)S(1)} %multiply_dynamic-update-slice_fusion.12, f32[8,128,128]{2,1,0:T(8,128)S(1)} %divide_multiply_fusion.3, bf16[8,16,128]{2,1,0:T(8,128)(2,1)S(1)} %get-tuple-element.102), kind=kOutput, calls=%fused_computation.154 | convolution fusion | flops 40108032 | bytes 1220608 | tf_op jit(solution)/shard_map/cond/branch_1_fun/ncb,nmab->cma/dot_general | solution.py:90
  42.4 3.7 %conditional.11 = (f32[16,9,128]{2,0,1:T(8,128)S(1)}) conditional(s32[]{:T(128)} %convert_element_type.114, () %tuple.51, (f32[3,128]{1,0:T(4,128)S(1)}, f32[3,128]{1,0:T(4,128)S(1)}, f32[3]{0:T(128)S(1)}, s32[]{:T(128)}, bf16[8,16,128]{2,1,0:T(8,128)(2,1)S(1)}) %tuple.115), branch_computations={%region_16.17_spmd, %region_17.19_spmd} | conditional | flops 41861136 | bytes 4435040 | solution.py:98
  43.5 1.8 %divide_multiply_fusion.5 = f32[8,128,128]{2,1,0:T(8,128)S(1)} fusion(f32[128,128]{1,0:T(8,128)S(1)} %get-tuple-element.155, f32[128,128]{1,0:T(8,128)S(1)} %get-tuple-element.154, f32[8]{0:T(128)S(1)} %add_multiply_fusion.5), kind=kLoop, calls=%fused_computation.255 | loop fusion | flops 524288 | bytes 655392 | tf_op jit(solution)/shard_map/cond/branch_1_fun/mul | solution.py:46
  45.3 0.7 %fusion.133 = f32[16,9,128]{2,0,1:T(8,128)S(1)} fusion(f32[9,128,128]{2,1,0:T(8,128)S(1)} %multiply_dynamic-update-slice_fusion.20, f32[8,128,128]{2,1,0:T(8,128)S(1)} %divide_multiply_fusion.5, bf16[8,16,128]{2,1,0:T(8,128)(2,1)S(1)} %get-tuple-element.112), kind=kOutput, calls=%fused_computation.254 | convolution fusion | flops 40108032 | bytes 1220608 | tf_op jit(solution)/shard_map/cond/branch_1_fun/ncb,nmab->cma/dot_general | solution.py:90
  46.1 3.7 %conditional.6 = (f32[16,9,128]{2,0,1:T(8,128)S(1)}) conditional(s32[]{:T(128)} %convert_element_type.104, () %tuple.41, (f32[3,128]{1,0:T(4,128)S(1)}, f32[3,128]{1,0:T(4,128)S(1)}, f32[3]{0:T(128)S(1)}, s32[]{:T(128)}, bf16[8,16,128]{2,1,0:T(8,128)(2,1)S(1)}) %tuple.116), branch_computations={%region_1.2_spmd, %region_2.4_spmd} | conditional | flops 41861136 | bytes 4435040 | solution.py:98
  47.3 1.8 %divide_multiply_fusion = f32[8,128,128]{2,1,0:T(8,128)S(1)} fusion(f32[128,128]{1,0:T(8,128)S(1)} %get-tuple-element.135, f32[128,128]{1,0:T(8,128)S(1)} %get-tuple-element.134, f32[8]{0:T(128)S(1)} %add_multiply_fusion), kind=kLoop, calls=%fused_computation.5 | loop fusion | flops 524288 | bytes 655392 | tf_op jit(solution)/shard_map/cond/branch_1_fun/mul | solution.py:46
  49.1 0.7 %fusion.3 = f32[16,9,128]{2,0,1:T(8,128)S(1)} fusion(f32[9,128,128]{2,1,0:T(8,128)S(1)} %multiply_dynamic-update-slice_fusion, f32[8,128,128]{2,1,0:T(8,128)S(1)} %divide_multiply_fusion, bf16[8,16,128]{2,1,0:T(8,128)(2,1)S(1)} %get-tuple-element.86), kind=kOutput, calls=%fused_computation.4 | convolution fusion | flops 40108032 | bytes 1220608 | tf_op jit(solution)/shard_map/cond/branch_1_fun/ncb,nmab->cma/dot_general | solution.py:90
  49.8 3.8 %conditional.7 = (f32[16,9,128]{2,0,1:T(8,128)S(1)}) conditional(s32[]{:T(128)} %convert_element_type.106, () %tuple.43, (f32[3,128]{1,0:T(4,128)S(1)}, f32[3,128]{1,0:T(4,128)S(1)}, f32[3]{0:T(128)S(1)}, s32[]{:T(128)}, bf16[8,16,128]{2,1,0:T(8,128)(2,1)S(1)}) %tuple.117), branch_computations={%region_4.5_spmd, %region_5.7_spmd} | conditional | flops 41861136 | bytes 4435040 | solution.py:98
  51.0 1.8 %divide_multiply_fusion.1 = f32[8,128,128]{2,1,0:T(8,128)S(1)} fusion(f32[128,128]{1,0:T(8,128)S(1)} %get-tuple-element.139, f32[128,128]{1,0:T(8,128)S(1)} %get-tuple-element.138, f32[8]{0:T(128)S(1)} %add_multiply_fusion.1), kind=kLoop, calls=%fused_computation.55 | loop fusion | flops 524288 | bytes 655392 | tf_op jit(solution)/shard_map/cond/branch_1_fun/mul | solution.py:46
  52.8 0.7 %fusion.29 = f32[16,9,128]{2,0,1:T(8,128)S(1)} fusion(f32[9,128,128]{2,1,0:T(8,128)S(1)} %multiply_dynamic-update-slice_fusion.4, f32[8,128,128]{2,1,0:T(8,128)S(1)} %divide_multiply_fusion.1, bf16[8,16,128]{2,1,0:T(8,128)(2,1)S(1)} %get-tuple-element.92), kind=kOutput, calls=%fused_computation.54 | convolution fusion | flops 40108032 | bytes 1220608 | tf_op jit(solution)/shard_map/cond/branch_1_fun/ncb,nmab->cma/dot_general | solution.py:90
  53.6 15.3 %all_gather.3 = f32[64,9,128]{2,0,1:T(8,128)S(1)} all-gather(f32[16,9,128]{2,0,1:T(8,128)S(1)} %add_multiply_fusion.6), channel_id=1, replica_groups=mesh['blk'=8,'chan'=4] {'chan'}, dimensions={0}, use_global_device_ids=true | all-gather | bytes 368640 | tf_op jit(solution)/shard_map/all_gather | solution.py:161
  (133 shorter events, 9.5 us)
Async XLA Ops:
  0.0 8.0 %copy-start = (f32[16,2]{0,1:T(2,128)S(1)}, f32[16,2]{0,1:T(2,128)}, u32[]{:S(2)}) copy-start(f32[16,2]{0,1:T(2,128)} %param.32) | copy-start | bytes 388
  0.0 16.8 %collective-permute-start.5 = (s32[128]{0:T(128)}, s32[128]{0:T(128)S(1)}, u32[]{:S(2)}, u32[]{:S(2)}) collective-permute-start(s32[128]{0:T(128)} %param.28), channel_id=1, source_target_pairs={{0,4},{4,8},{8,12},{12,16},{16,20},{20,24},{24,28},{28,0},{1,5},{5... | collective-permute-start | bytes 1544 | tf_op jit(solution)/shard_map/ppermute | solution.py:15
  0.5 17.1 %collective-permute-start.2 = (s32[128]{0:T(128)}, s32[128]{0:T(128)S(1)}, u32[]{:S(2)}, u32[]{:S(2)}) collective-permute-start(s32[128]{0:T(128)} %param.28), channel_id=1, source_target_pairs={{0,28},{4,0},{8,4},{12,8},{16,12},{20,16},{24,20},{28,24},{1,29},{... | collective-permute-start | bytes 1544 | tf_op jit(solution)/shard_map/ppermute | solution.py:15
  3.4 9.5 %collective-permute-start = (f32[3,128]{1,0:T(4,128)}, f32[3,128]{1,0:T(4,128)S(1)}, u32[]{:S(2)}, u32[]{:S(2)}) collective-permute-start(f32[3,128]{1,0:T(4,128)} %param.27), channel_id=1, source_target_pairs={{0,28},{4,0},{8,4},{12,8},{16,12},{20,16},{24,20},{28,24},{1,29},{... | collective-permute-start | bytes 4616 | tf_op jit(solution)/shard_map/ppermute | solution.py:15
  4.1 10.8 %collective-permute-start.3 = (f32[3,128]{1,0:T(4,128)}, f32[3,128]{1,0:T(4,128)S(1)}, u32[]{:S(2)}, u32[]{:S(2)}) collective-permute-start(f32[3,128]{1,0:T(4,128)} %param.27), channel_id=1, source_target_pairs={{0,4},{4,8},{8,12},{12,16},{16,20},{20,24},{24,28},{28,0},{1,5},{5... | collective-permute-start | bytes 4616 | tf_op jit(solution)/shard_map/ppermute | solution.py:15
  4.1 19.9 %collective-permute-start.4 = (f32[16,128]{1,0:T(8,128)}, f32[16,128]{1,0:T(8,128)S(1)}, u32[]{:S(2)}, u32[]{:S(2)}) collective-permute-start(f32[16,128]{1,0:T(8,128)} %param.29), channel_id=1, source_target_pairs={{0,4},{4,8},{8,12},{12,16},{16,20},{20,24},{24,28},{28,0},{1,5},{5... | collective-permute-start | bytes 24584 | tf_op jit(solution)/shard_map/ppermute | solution.py:15
  5.9 0.7 copy-start.4
  5.9 2.1 %copy-start.6 = (f32[16,128]{1,0:T(8,128)S(1)}, f32[16,128]{1,0:T(8,128)}, u32[]{:S(2)}) copy-start(f32[16,128]{1,0:T(8,128)} %param.29) | copy-start | bytes 24580
  5.9 2.1 %copy-start.8 = (s32[128]{0:T(128)S(1)}, s32[128]{0:T(128)}, u32[]{:S(2)}) copy-start(s32[128]{0:T(128)} %param.28) | copy-start | bytes 1540
  6.0 2.2 %copy-start.7 = (f32[16,2]{0,1:T(2,128)S(1)}, f32[16,2]{0,1:T(2,128)}, u32[]{:S(2)}) copy-start(f32[16,2]{0,1:T(2,128)} %param.33) | copy-start | bytes 388
  6.0 2.4 %copy-start.2 = (f32[3,64,64]{2,1,0:T(8,128)S(1)}, f32[3,64,64]{2,1,0:T(8,128)}, u32[]{:S(2)}) copy-start(f32[3,64,64]{2,1,0:T(8,128)} %param.34) | copy-start | bytes 147460
  7.9 2.3 %copy-start.5 = (f32[8,16]{1,0:T(8,128)S(1)}, f32[8,16]{1,0:T(8,128)}, u32[]{:S(2)}) copy-start(f32[8,16]{1,0:T(8,128)} %param.31) | copy-start | bytes 1540
  11.0 23.1 %copy-start.1 = (f32[3,128]{1,0:T(4,128)S(1)}, f32[3,128]{1,0:T(4,128)}, u32[]{:S(2)}) copy-start(f32[3,128]{1,0:T(4,128)} %param.27) | copy-start | bytes 4612
  11.0 23.2 %copy-start.3 = (f32[3]{0:T(128)S(1)}, f32[3]{0:T(128)}, u32[]{:S(2)}) copy-start(f32[3]{0:T(128)} %constant.182.clone) | copy-start | bytes 40
  13.0 8.9 %collective-permute-start.6 = (f32[3,128]{1,0:T(4,128)S(1)}, f32[3,128]{1,0:T(4,128)S(1)}, u32[]{:S(2)}, u32[]{:S(2)}) collective-permute-start(f32[3,128]{1,0:T(4,128)S(1)} %collective-permute-done), channel_id=1, source_target_pairs={{0,28},{4,0},{8,4},{12,8},{16,12},{20,16},{24,20},{28,24},{1,29},{... | collective-permute-start | bytes 4616 | tf_op jit(solution)/shard_map/ppermute | solution.py:15
  14.9 8.6 %collective-permute-start.9 = (f32[3,128]{1,0:T(4,128)S(1)}, f32[3,128]{1,0:T(4,128)}, u32[]{:S(2)}, u32[]{:S(2)}) collective-permute-start(f32[3,128]{1,0:T(4,128)S(1)} %collective-permute-done.3), channel_id=1, source_target_pairs={{0,4},{4,8},{8,12},{12,16},{16,20},{20,24},{24,28},{28,0},{1,5},{5... | collective-permute-start | bytes 4616 | tf_op jit(solution)/shard_map/ppermute | solution.py:15
  16.8 3.9 %collective-permute-start.11 = (s32[128]{0:T(128)S(1)}, s32[128]{0:T(128)S(1)}, u32[]{:S(2)}, u32[]{:S(2)}) collective-permute-start(s32[128]{0:T(128)S(1)} %collective-permute-done.5), channel_id=1, source_target_pairs={{0,4},{4,8},{8,12},{12,16},{16,20},{20,24},{24,28},{28,0},{1,5},{5... | collective-permute-start | bytes 1544 | tf_op jit(solution)/shard_map/ppermute | solution.py:15
  17.6 3.3 %collective-permute-start.8 = (s32[128]{0:T(128)S(1)}, s32[128]{0:T(128)S(1)}, u32[]{:S(2)}, u32[]{:S(2)}) collective-permute-start(s32[128]{0:T(128)S(1)} %collective-permute-done.2), channel_id=1, source_target_pairs={{0,28},{4,0},{8,4},{12,8},{16,12},{20,16},{24,20},{28,24},{1,29},{... | collective-permute-start | bytes 1544 | tf_op jit(solution)/shard_map/ppermute | solution.py:15
  20.8 3.5 %collective-permute-start.1 = (f32[16,128]{1,0:T(8,128)S(1)}, f32[16,128]{1,0:T(8,128)S(1)}, u32[]{:S(2)}, u32[]{:S(2)}) collective-permute-start(f32[16,128]{1,0:T(8,128)S(1)} %copy-done.6), channel_id=1, source_target_pairs={{0,28},{4,0},{8,4},{12,8},{16,12},{20,16},{24,20},{28,24},{1,29},{... | collective-permute-start | bytes 24584 | tf_op jit(solution)/shard_map/ppermute | solution.py:15
  20.9 9.4 %collective-permute-start.17 = (s32[128]{0:T(128)S(1)}, s32[128]{0:T(128)S(1)}, u32[]{:S(2)}, u32[]{:S(2)}) collective-permute-start(s32[128]{0:T(128)S(1)} %collective-permute-done.11), channel_id=1, source_target_pairs={{0,4},{4,8},{8,12},{12,16},{16,20},{20,24},{24,28},{28,0},{1,5},{5... | collective-permute-start | bytes 1544 | tf_op jit(solution)/shard_map/ppermute | solution.py:15
  21.9 11.9 %collective-permute-start.14 = (s32[128]{0:T(128)S(1)}, s32[128]{0:T(128)S(1)}, u32[]{:S(2)}, u32[]{:S(2)}) collective-permute-start(s32[128]{0:T(128)S(1)} %collective-permute-done.8), channel_id=1, source_target_pairs={{0,28},{4,0},{8,4},{12,8},{16,12},{20,16},{24,20},{28,24},{1,29},{... | collective-permute-start | bytes 1544 | tf_op jit(solution)/shard_map/ppermute | solution.py:15
  23.5 10.6 %collective-permute-start.12 = (f32[3,128]{1,0:T(4,128)S(1)}, f32[3,128]{1,0:T(4,128)S(1)}, u32[]{:S(2)}, u32[]{:S(2)}) collective-permute-start(f32[3,128]{1,0:T(4,128)S(1)} %collective-permute-done.6), channel_id=1, source_target_pairs={{0,28},{4,0},{8,4},{12,8},{16,12},{20,16},{24,20},{28,24},{1,29},{... | collective-permute-start | bytes 4616 | tf_op jit(solution)/shard_map/ppermute | solution.py:15
  24.0 18.4 %collective-permute-start.15 = (f32[3,128]{1,0:T(4,128)}, f32[3,128]{1,0:T(4,128)S(1)}, u32[]{:S(2)}, u32[]{:S(2)}) collective-permute-start(f32[3,128]{1,0:T(4,128)} %collective-permute-done.9), channel_id=1, source_target_pairs={{0,4},{4,8},{8,12},{12,16},{16,20},{20,24},{24,28},{28,0},{1,5},{5... | collective-permute-start | bytes 4616 | tf_op jit(solution)/shard_map/ppermute | solution.py:15
  24.2 4.0 %collective-permute-start.10 = (f32[16,128]{1,0:T(8,128)S(1)}, f32[16,128]{1,0:T(8,128)S(1)}, u32[]{:S(2)}, u32[]{:S(2)}) collective-permute-start(f32[16,128]{1,0:T(8,128)S(1)} %collective-permute-done.4), channel_id=1, source_target_pairs={{0,4},{4,8},{8,12},{12,16},{16,20},{20,24},{24,28},{28,0},{1,5},{5... | collective-permute-start | bytes 24584 | tf_op jit(solution)/shard_map/ppermute | solution.py:15
  28.2 1.4 %collective-permute-start.7 = (f32[16,128]{1,0:T(8,128)S(1)}, f32[16,128]{1,0:T(8,128)S(1)}, u32[]{:S(2)}, u32[]{:S(2)}) collective-permute-start(f32[16,128]{1,0:T(8,128)S(1)} %collective-permute-done.1), channel_id=1, source_target_pairs={{0,28},{4,0},{8,4},{12,8},{16,12},{20,16},{24,20},{28,24},{1,29},{... | collective-permute-start | bytes 24584 | tf_op jit(solution)/shard_map/ppermute | solution.py:15
  29.6 4.0 %collective-permute-start.16 = (f32[16,128]{1,0:T(8,128)S(1)}, f32[16,128]{1,0:T(8,128)S(1)}, u32[]{:S(2)}, u32[]{:S(2)}) collective-permute-start(f32[16,128]{1,0:T(8,128)S(1)} %collective-permute-done.10), channel_id=1, source_target_pairs={{0,4},{4,8},{8,12},{12,16},{16,20},{20,24},{24,28},{28,0},{1,5},{5... | collective-permute-start | bytes 24584 | tf_op jit(solution)/shard_map/ppermute | solution.py:15
  30.3 3.5 %collective-permute-start.13 = (f32[16,128]{1,0:T(8,128)S(1)}, f32[16,128]{1,0:T(8,128)S(1)}, u32[]{:S(2)}, u32[]{:S(2)}) collective-permute-start(f32[16,128]{1,0:T(8,128)S(1)} %collective-permute-done.7), channel_id=1, source_target_pairs={{0,28},{4,0},{8,4},{12,8},{16,12},{20,16},{24,20},{28,24},{1,29},{... | collective-permute-start | bytes 24584 | tf_op jit(solution)/shard_map/ppermute | solution.py:15
where the time goes:
time: 70.3 us; the launch traced here: 70 us
  starting transfers between devices  16.1 us (23%)
  other arithmetic  15.8 us (22%)
  blocking collectives  15.3 us (22%)
  waiting for transfers between devices  6.81 us (10%)
  matrix products  6.24 us (9%)
  between operations  4.81 us (7%)
  loops' own time  3.71 us (5%)
  local copies, waits for them, and re-layouts  1.22 us (2%)
    ppermute x18, starting transfers between devices, from_behind(): lax.ppermute(value, axis, [(i, (i + by) % size) for i in range(size)])  16.1 us
    all_gather x1, blocking collectives, shards(): lax.all_gather(features, 'chan', axis=0, tiled=True)  15.3 us
    mul x6, other arithmetic, table_of(): math.sqrt(2.0 / cut_radius)  10.8 us
    ppermute x18, waiting for transfers between devices, from_behind(): lax.ppermute(value, axis, [(i, (i + by) % size) for i in range(size)])  6.81 us
    another operation x6, loops' own time, contributions(): return lax.cond(active > 0, compute, skipped)  3.71 us
    dot_general x5, matrix products, compute(): jnp.einsum('ncb,nmab->cma', other_carried, pair_table, preferred_element_...  3.65 us
    reduce_sum x6, other arithmetic, table_of(): distance = jnp.sqrt(jnp.sum(separation * separation, axis=0) + soften)  2.27 us
  transfers between devices with their start and end apart: 18, of which 6 were waited for; matrix products, arithmetic and copies ran while one was open for 18% of the time, Pallas kernels for 0%

commit v1 on v0

--- a/solution.py
+++ b/solution.py
@@ -8,6 +8,23 @@
 cross_width = 48.0
 cut_radius = 5.0
 soften = 0.25
+
+
+def in_order(blocks, dim):
+    blocks = jnp.moveaxis(blocks, 0, dim)
+    dims = blocks.shape
+    return blocks.reshape(*dims[:dim], dims[dim] * dims[dim + 1], *dims[dim + 2 :])
+
+
+def ring_gather(shard, axis, dim):
+    length = lax.axis_size(axis)
+    right = [(i, (i + 1) % length) for i in range(length)]
+    pieces = [shard]
+    while len(pieces) < length:
+        pieces.append(lax.ppermute(pieces[-1], axis, right))
+    index = lax.axis_index(axis)
+    pieces = jnp.stack(pieces)[(index - jnp.arange(length)) % length]
+    return in_order(pieces, dim)
 
 
 def from_behind(value, axis, by):
@@ -158,7 +175,7 @@
     mixed_tensor = jnp.einsum(
         "mpc,cma->pma",
         weights_out,
-        lax.all_gather(features, "chan", axis=0, tiled=True),
+        ring_gather(features, "chan", 0),
         precision=lax.Precision.HIGHEST,
     )
     return describe(mixed_tensor)

time: 70.3 us -> 73.9 us (1.051)
  waiting for transfers between devices: 6.81 us -> 23.1 us
  blocking collectives: 15.3 us -> 0 us
  starting transfers between devices: 16.1 us -> 18.3 us
    ppermute x0 -> x3, waiting for transfers between devices: none -> 17 us  [ring_gather(): pieces.append(lax.ppermute(pieces[-1], axis, right))]
    all_gather x1 -> x0, blocking collectives: 15.3 us -> none  [shards(): lax.all_gather(features, 'chan', axis=0, tiled=True)]
    ppermute x0 -> x3, starting transfers between devices: none -> 2.16 us  [ring_gather(): pieces.append(lax.ppermute(pieces[-1], axis, right))]
    ppermute x18, waiting for transfers between devices: 6.81 us -> 6 us  [from_behind(): lax.ppermute(value, axis, [(i, (i + by) % size) for i in range(size)])]
  transfers between devices with their start and end apart: 18 -> 21, of which waited for: 6 -> 7; matrix products, arithmetic and copies ran while one was open for 18% -> 17% of each run, Pallas kernels for 0% -> 0%
where the time goes in v1:
time: 73.9 us; the launch traced here: 73.6 us
  waiting for transfers between devices  23.1 us (31%)
  starting transfers between devices  18.3 us (25%)
  other arithmetic  15.8 us (21%)
  matrix products  6.25 us (8%)
  between operations  4.75 us (6%)
  loops' own time  3.69 us (5%)
  local copies, waits for them, and re-layouts  1.78 us (2%)
    ppermute x3, waiting for transfers between devices, ring_gather(): pieces.append(lax.ppermute(pieces[-1], axis, right))  17 us
    ppermute x18, starting transfers between devices, from_behind(): lax.ppermute(value, axis, [(i, (i + by) % size) for i in range(size)])  16.1 us
    mul x6, other arithmetic, table_of(): math.sqrt(2.0 / cut_radius)  10.8 us
    ppermute x18, waiting for transfers between devices, from_behind(): lax.ppermute(value, axis, [(i, (i + by) % size) for i in range(size)])  6 us
    another operation x6, loops' own time, contributions(): return lax.cond(active > 0, compute, skipped)  3.69 us
    dot_general x5, matrix products, compute(): jnp.einsum('ncb,nmab->cma', other_carried, pair_table, preferred_element_...  3.66 us
    reduce_sum x6, other arithmetic, table_of(): distance = jnp.sqrt(jnp.sum(separation * separation, axis=0) + soften)  2.23 us
    ppermute x3, starting transfers between devices, ring_gather(): pieces.append(lax.ppermute(pieces[-1], axis, right))  2.16 us
  transfers between devices with their start and end apart: 21, of which 7 were waited for; matrix products, arithmetic and copies ran while one was open for 17% of the time, Pallas kernels for 0%

profile of v1, /device:TPU:0, one launch (start us, length us, event | category | flops | bytes accessed | tf_op | source)
XLA Modules:
  0.0 73.6 jit_solution(138974212127674714)
XLA Ops:
  0.5 2.9 %collective-permute-start.2 = (s32[128]{0:T(128)}, s32[128]{0:T(128)S(1)}, u32[]{:S(2)}, u32[]{:S(2)}) collective-permute-start(s32[128]{0:T(128)} %param.28), channel_id=1, source_target_pairs={{0,28},{4,0},{8,4},{12,8},{16,12},{20,16},{24,20},{28,24},{1,29},{... | collective-permute-start | bytes 1544 | tf_op jit(solution)/shard_map/ppermute | solution.py:32
  4.1 0.8 %collective-permute-start.4 = (f32[16,128]{1,0:T(8,128)}, f32[16,128]{1,0:T(8,128)S(1)}, u32[]{:S(2)}, u32[]{:S(2)}) collective-permute-start(f32[16,128]{1,0:T(8,128)} %param.29), channel_id=1, source_target_pairs={{0,4},{4,8},{8,12},{12,16},{16,20},{20,24},{24,28},{28,0},{1,5},{5... | collective-permute-start | bytes 24584 | tf_op jit(solution)/shard_map/ppermute | solution.py:32
  4.9 0.9 %multiply_reduce_fusion.6 = (f32[128,128]{1,0:T(8,128)S(1)}, f32[3,128,128]{2,1,0:T(8,128)S(1)}) fusion(f32[3]{0:T(128)} %constant.244, f32[3]{0:T(128)} %constant.242.clone, f32[3,128]{1,0:T(4,128)} %param.27), kind=kLoop, calls=%fused_computation.333 | loop fusion | flops 376832 | bytes 263704 | tf_op jit(solution)/shard_map/reduce_sum | solution.py:39
  8.3 1.8 %divide_multiply_fusion.6 = f32[8,128,128]{2,1,0:T(8,128)S(1)} fusion(f32[128,128]{1,0:T(8,128)S(1)} %get-tuple-element.162, f32[128,128]{1,0:T(8,128)S(1)} %get-tuple-element.161, f32[8]{0:T(128)S(1)} %add_multiply_fusion.7), kind=kLoop, calls=%fused_computation.323 | loop fusion | flops 524288 | bytes 655392 | tf_op jit(solution)/shard_map/mul | solution.py:63
  10.2 0.7 %fusion.159 = f32[16,9,128]{2,0,1:T(8,128)S(1)} fusion(f32[9,128,128]{2,1,0:T(8,128)S(1)} %multiply_dynamic-update-slice_fusion.24, f32[8,128,128]{2,1,0:T(8,128)S(1)} %divide_multiply_fusion.6, f32[16,128]{1,0:T(8,128)S(1)} %fusion.167, f32[8,16]{1,0:T(8,128)S(1)} %copy-done.5), kind=kOutput, calls=%fused_computation.306 | convolution fusion | flops 40140800 | bytes 1196544 | tf_op jit(solution)/shard_map/ncb,nmab->cma/dot_general | solution.py:150
  11.6 1.9 %collective-permute-start.6 = (f32[3,128]{1,0:T(4,128)S(1)}, f32[3,128]{1,0:T(4,128)S(1)}, u32[]{:S(2)}, u32[]{:S(2)}) collective-permute-start(f32[3,128]{1,0:T(4,128)S(1)} %collective-permute-done), channel_id=1, source_target_pairs={{0,28},{4,0},{8,4},{12,8},{16,12},{20,16},{24,20},{28,24},{1,29},{... | collective-permute-start | bytes 4616 | tf_op jit(solution)/shard_map/ppermute | solution.py:32
  15.4 0.7 %collective-permute-start.11 = (s32[128]{0:T(128)S(1)}, s32[128]{0:T(128)S(1)}, u32[]{:S(2)}, u32[]{:S(2)}) collective-permute-start(s32[128]{0:T(128)S(1)} %collective-permute-done.5), channel_id=1, source_target_pairs={{0,4},{4,8},{8,12},{12,16},{16,20},{20,24},{24,28},{28,0},{1,5},{5... | collective-permute-start | bytes 1544 | tf_op jit(solution)/shard_map/ppermute | solution.py:32
  16.2 2.0 %collective-permute-start.8 = (s32[128]{0:T(128)S(1)}, s32[128]{0:T(128)S(1)}, u32[]{:S(2)}, u32[]{:S(2)}) collective-permute-start(s32[128]{0:T(128)S(1)} %collective-permute-done.2), channel_id=1, source_target_pairs={{0,28},{4,0},{8,4},{12,8},{16,12},{20,16},{24,20},{28,24},{1,29},{... | collective-permute-start | bytes 1544 | tf_op jit(solution)/shard_map/ppermute | solution.py:32
  20.5 2.1 %collective-permute-start.14 = (s32[128]{0:T(128)S(1)}, s32[128]{0:T(128)S(1)}, u32[]{:S(2)}, u32[]{:S(2)}) collective-permute-start(s32[128]{0:T(128)S(1)} %collective-permute-done.8), channel_id=1, source_target_pairs={{0,28},{4,0},{8,4},{12,8},{16,12},{20,16},{24,20},{28,24},{1,29},{... | collective-permute-start | bytes 1544 | tf_op jit(solution)/shard_map/ppermute | solution.py:32
  23.7 3.6 %collective-permute-done.10 = f32[16,128]{1,0:T(8,128)S(1)} collective-permute-done((f32[16,128]{1,0:T(8,128)S(1)}, f32[16,128]{1,0:T(8,128)S(1)}, u32[]{:S(2)}, u32[]{:S(2)}) %collective-permute-start.10) | collective-permute-done | bytes 8224 | tf_op jit(solution)/shard_map/ppermute | solution.py:32
  27.5 1.2 %collective-permute-done.7 = f32[16,128]{1,0:T(8,128)S(1)} collective-permute-done((f32[16,128]{1,0:T(8,128)S(1)}, f32[16,128]{1,0:T(8,128)S(1)}, u32[]{:S(2)}, u32[]{:S(2)}) %collective-permute-start.7) | collective-permute-done | bytes 8224 | tf_op jit(solution)/shard_map/ppermute | solution.py:32
  29.0 2.6 %collective-permute-start.13 = (f32[16,128]{1,0:T(8,128)S(1)}, f32[16,128]{1,0:T(8,128)S(1)}, u32[]{:S(2)}, u32[]{:S(2)}) collective-permute-start(f32[16,128]{1,0:T(8,128)S(1)} %collective-permute-done.7), channel_id=1, source_target_pairs={{0,28},{4,0},{8,4},{12,8},{16,12},{20,16},{24,20},{28,24},{1,29},{... | collective-permute-start | bytes 24584 | tf_op jit(solution)/shard_map/ppermute | solution.py:32
  31.6 1.1 %collective-permute-done.16 = f32[16,128]{1,0:T(8,128)S(1)} collective-permute-done((f32[16,128]{1,0:T(8,128)S(1)}, f32[16,128]{1,0:T(8,128)S(1)}, u32[]{:S(2)}, u32[]{:S(2)}) %collective-permute-start.16) | collective-permute-done | bytes 8224 | tf_op jit(solution)/shard_map/ppermute | solution.py:32
  33.3 3.7 %conditional.8 = (f32[16,9,128]{2,0,1:T(8,128)S(1)}) conditional(s32[]{:T(128)} %convert_element_type.108, () %tuple.45, (f32[3,128]{1,0:T(4,128)S(1)}, f32[3,128]{1,0:T(4,128)S(1)}, f32[3]{0:T(128)S(1)}, s32[]{:T(128)}, bf16[8,16,128]{2,1,0:T(8,128)(2,1)S(1)}) %tuple.113), branch_computations={%region_7.8_spmd, %region_8.10_spmd} | conditional | flops 41861136 | bytes 4435040 | solution.py:115
  34.5 1.8 %divide_multiply_fusion.2 = f32[8,128,128]{2,1,0:T(8,128)S(1)} fusion(f32[128,128]{1,0:T(8,128)S(1)} %get-tuple-element.143, f32[128,128]{1,0:T(8,128)S(1)} %get-tuple-element.142, f32[8]{0:T(128)S(1)} %add_multiply_fusion.2), kind=kLoop, calls=%fused_computation.106 | loop fusion | flops 524288 | bytes 655392 | tf_op jit(solution)/shard_map/cond/branch_1_fun/mul | solution.py:63
  36.3 0.7 fusion.55
  37.0 4.4 %conditional.9 = (f32[16,9,128]{2,0,1:T(8,128)S(1)}) conditional(s32[]{:T(128)} %convert_element_type.110, () %tuple.47, (f32[3,128]{1,0:T(4,128)}, f32[3,128]{1,0:T(4,128)S(1)}, f32[3]{0:T(128)S(1)}, s32[]{:T(128)}, bf16[8,16,128]{2,1,0:T(8,128)(2,1)S(1)}) %tuple.114), branch_computations={%region_10.11_spmd, %region_11.13_spmd} | conditional | flops 41861136 | bytes 4435040 | solution.py:115
  37.1 0.8 %multiply_reduce_fusion.3 = (f32[128,128]{1,0:T(8,128)S(1)}, f32[3,128,128]{2,1,0:T(8,128)S(1)}) fusion(f32[3]{0:T(128)S(1)} %get-tuple-element.100, f32[3,128]{1,0:T(4,128)S(1)} %get-tuple-element.99, f32[3,128]{1,0:T(4,128)} %get-tuple-element.98), kind=kLoop, calls=%fused_computation.162 | loop fusion | flops 376832 | bytes 265228 | tf_op jit(solution)/shard_map/cond/branch_1_fun/reduce_sum | solution.py:39
  38.9 1.8 %divide_multiply_fusion.3 = f32[8,128,128]{2,1,0:T(8,128)S(1)} fusion(f32[128,128]{1,0:T(8,128)S(1)} %get-tuple-element.147, f32[128,128]{1,0:T(8,128)S(1)} %get-tuple-element.146, f32[8]{0:T(128)S(1)} %add_multiply_fusion.3), kind=kLoop, calls=%fused_computation.156 | loop fusion | flops 524288 | bytes 655392 | tf_op jit(solution)/shard_map/cond/branch_1_fun/mul | solution.py:63
  40.7 0.7 fusion.81
  41.4 3.7 %conditional.11 = (f32[16,9,128]{2,0,1:T(8,128)S(1)}) conditional(s32[]{:T(128)} %convert_element_type.114, () %tuple.51, (f32[3,128]{1,0:T(4,128)S(1)}, f32[3,128]{1,0:T(4,128)S(1)}, f32[3]{0:T(128)S(1)}, s32[]{:T(128)}, bf16[8,16,128]{2,1,0:T(8,128)(2,1)S(1)}) %tuple.115), branch_computations={%region_16.17_spmd, %region_17.19_spmd} | conditional | flops 41861136 | bytes 4435040 | solution.py:115
  42.6 1.8 %divide_multiply_fusion.5 = f32[8,128,128]{2,1,0:T(8,128)S(1)} fusion(f32[128,128]{1,0:T(8,128)S(1)} %get-tuple-element.155, f32[128,128]{1,0:T(8,128)S(1)} %get-tuple-element.154, f32[8]{0:T(128)S(1)} %add_multiply_fusion.5), kind=kLoop, calls=%fused_computation.256 | loop fusion | flops 524288 | bytes 655392 | tf_op jit(solution)/shard_map/cond/branch_1_fun/mul | solution.py:63
  44.4 0.7 fusion.133
  45.1 3.7 %conditional.6 = (f32[16,9,128]{2,0,1:T(8,128)S(1)}) conditional(s32[]{:T(128)} %convert_element_type.104, () %tuple.41, (f32[3,128]{1,0:T(4,128)S(1)}, f32[3,128]{1,0:T(4,128)S(1)}, f32[3]{0:T(128)S(1)}, s32[]{:T(128)}, bf16[8,16,128]{2,1,0:T(8,128)(2,1)S(1)}) %tuple.116), branch_computations={%region_1.2_spmd, %region_2.4_spmd} | conditional | flops 41861136 | bytes 4435040 | solution.py:115
  46.3 1.8 %divide_multiply_fusion = f32[8,128,128]{2,1,0:T(8,128)S(1)} fusion(f32[128,128]{1,0:T(8,128)S(1)} %get-tuple-element.135, f32[128,128]{1,0:T(8,128)S(1)} %get-tuple-element.134, f32[8]{0:T(128)S(1)} %add_multiply_fusion), kind=kLoop, calls=%fused_computation.6 | loop fusion | flops 524288 | bytes 655392 | tf_op jit(solution)/shard_map/cond/branch_1_fun/mul | solution.py:63
  48.9 3.7 %conditional.7 = (f32[16,9,128]{2,0,1:T(8,128)S(1)}) conditional(s32[]{:T(128)} %convert_element_type.106, () %tuple.43, (f32[3,128]{1,0:T(4,128)S(1)}, f32[3,128]{1,0:T(4,128)S(1)}, f32[3]{0:T(128)S(1)}, s32[]{:T(128)}, bf16[8,16,128]{2,1,0:T(8,128)(2,1)S(1)}) %tuple.117), branch_computations={%region_4.5_spmd, %region_5.7_spmd} | conditional | flops 41861136 | bytes 4435040 | solution.py:115
  50.1 1.8 %divide_multiply_fusion.1 = f32[8,128,128]{2,1,0:T(8,128)S(1)} fusion(f32[128,128]{1,0:T(8,128)S(1)} %get-tuple-element.139, f32[128,128]{1,0:T(8,128)S(1)} %get-tuple-element.138, f32[8]{0:T(128)S(1)} %add_multiply_fusion.1), kind=kLoop, calls=%fused_computation.56 | loop fusion | flops 524288 | bytes 655392 | tf_op jit(solution)/shard_map/cond/branch_1_fun/mul | solution.py:63
  51.9 0.7 fusion.29
  52.7 2.2 %collective-permute-start.18 = (f32[16,9,128]{2,0,1:T(8,128)S(1)}, f32[16,9,128]{2,0,1:T(8,128)S(1)}, u32[]{:S(2)}, u32[]{:S(2)}) collective-permute-start(f32[16,9,128]{2,0,1:T(8,128)S(1)} %add_multiply_fusion.6), channel_id=1, source_target_pairs={{0,1},{1,2},{2,3},{3,0},{4,5},{5,6},{6,7},{7,4},{8,9},{9,10},{10,1... | collective-permute-start | bytes 221192 | tf_op jit(solution)/shard_map/ppermute | solution.py:24
  54.8 4.5 %collective-permute-done.18 = f32[16,9,128]{2,0,1:T(8,128)S(1)} collective-permute-done((f32[16,9,128]{2,0,1:T(8,128)S(1)}, f32[16,9,128]{2,0,1:T(8,128)S(1)}, u32[]{:S(2)}, u32[]{:S(2)}) %collective-permute-start.18) | collective-permute-done | bytes 73760 | tf_op jit(solution)/shard_map/ppermute | solution.py:24
  59.4 6.4 %collective-permute-done.19 = f32[16,9,128]{2,0,1:T(8,128)S(1)} collective-permute-done((f32[16,9,128]{2,0,1:T(8,128)S(1)}, f32[16,9,128]{2,0,1:T(8,128)S(1)}, u32[]{:S(2)}, u32[]{:S(2)}) %collective-permute-start.19) | collective-permute-done | bytes 73760 | tf_op jit(solution)/shard_map/ppermute | solution.py:24
  65.8 6.1 %collective-permute-done.20 = f32[16,9,128]{2,0,1:T(8,128)S(1)} collective-permute-done((f32[16,9,128]{2,0,1:T(8,128)S(1)}, f32[16,9,128]{2,0,1:T(8,128)S(1)}, u32[]{:S(2)}, u32[]{:S(2)}) %collective-permute-start.20) | collective-permute-done | bytes 73760 | tf_op jit(solution)/shard_map/ppermute | solution.py:24
  (143 shorter events, 10.8 us)
Async XLA Ops:
  0.0 7.9 %copy-start = (f32[16,2]{0,1:T(2,128)S(1)}, f32[16,2]{0,1:T(2,128)}, u32[]{:S(2)}) copy-start(f32[16,2]{0,1:T(2,128)} %param.32) | copy-start | bytes 388
  0.0 15.4 %collective-permute-start.5 = (s32[128]{0:T(128)}, s32[128]{0:T(128)S(1)}, u32[]{:S(2)}, u32[]{:S(2)}) collective-permute-start(s32[128]{0:T(128)} %param.28), channel_id=1, source_target_pairs={{0,4},{4,8},{8,12},{12,16},{16,20},{20,24},{24,28},{28,0},{1,5},{5... | collective-permute-start | bytes 1544 | tf_op jit(solution)/shard_map/ppermute | solution.py:32
  0.5 15.7 %collective-permute-start.2 = (s32[128]{0:T(128)}, s32[128]{0:T(128)S(1)}, u32[]{:S(2)}, u32[]{:S(2)}) collective-permute-start(s32[128]{0:T(128)} %param.28), channel_id=1, source_target_pairs={{0,28},{4,0},{8,4},{12,8},{16,12},{20,16},{24,20},{28,24},{1,29},{... | collective-permute-start | bytes 1544 | tf_op jit(solution)/shard_map/ppermute | solution.py:32
  3.4 8.2 %collective-permute-start = (f32[3,128]{1,0:T(4,128)}, f32[3,128]{1,0:T(4,128)S(1)}, u32[]{:S(2)}, u32[]{:S(2)}) collective-permute-start(f32[3,128]{1,0:T(4,128)} %param.27), channel_id=1, source_target_pairs={{0,28},{4,0},{8,4},{12,8},{16,12},{20,16},{24,20},{28,24},{1,29},{... | collective-permute-start | bytes 4616 | tf_op jit(solution)/shard_map/ppermute | solution.py:32
  4.1 9.5 %collective-permute-start.3 = (f32[3,128]{1,0:T(4,128)}, f32[3,128]{1,0:T(4,128)S(1)}, u32[]{:S(2)}, u32[]{:S(2)}) collective-permute-start(f32[3,128]{1,0:T(4,128)} %param.27), channel_id=1, source_target_pairs={{0,4},{4,8},{8,12},{12,16},{16,20},{20,24},{24,28},{28,0},{1,5},{5... | collective-permute-start | bytes 4616 | tf_op jit(solution)/shard_map/ppermute | solution.py:32
  4.1 18.6 %collective-permute-start.4 = (f32[16,128]{1,0:T(8,128)}, f32[16,128]{1,0:T(8,128)S(1)}, u32[]{:S(2)}, u32[]{:S(2)}) collective-permute-start(f32[16,128]{1,0:T(8,128)} %param.29), channel_id=1, source_target_pairs={{0,4},{4,8},{8,12},{12,16},{16,20},{20,24},{24,28},{28,0},{1,5},{5... | collective-permute-start | bytes 24584 | tf_op jit(solution)/shard_map/ppermute | solution.py:32
  5.9 0.7 copy-start.4
  5.9 2.0 %copy-start.6 = (f32[16,128]{1,0:T(8,128)S(1)}, f32[16,128]{1,0:T(8,128)}, u32[]{:S(2)}) copy-start(f32[16,128]{1,0:T(8,128)} %param.29) | copy-start | bytes 24580
  5.9 2.0 %copy-start.8 = (s32[128]{0:T(128)S(1)}, s32[128]{0:T(128)}, u32[]{:S(2)}) copy-start(s32[128]{0:T(128)} %param.28) | copy-start | bytes 1540
  6.0 2.1 %copy-start.7 = (f32[16,2]{0,1:T(2,128)S(1)}, f32[16,2]{0,1:T(2,128)}, u32[]{:S(2)}) copy-start(f32[16,2]{0,1:T(2,128)} %param.33) | copy-start | bytes 388
  6.1 4.1 %copy-start.5 = (f32[8,16]{1,0:T(8,128)S(1)}, f32[8,16]{1,0:T(8,128)}, u32[]{:S(2)}) copy-start(f32[8,16]{1,0:T(8,128)} %param.31) | copy-start | bytes 1540
  10.9 22.3 %copy-start.1 = (f32[3,128]{1,0:T(4,128)S(1)}, f32[3,128]{1,0:T(4,128)}, u32[]{:S(2)}) copy-start(f32[3,128]{1,0:T(4,128)} %param.27) | copy-start | bytes 4612
  10.9 22.3 %copy-start.3 = (f32[3]{0:T(128)S(1)}, f32[3]{0:T(128)}, u32[]{:S(2)}) copy-start(f32[3]{0:T(128)} %constant.242.clone) | copy-start | bytes 40
  11.6 8.9 %collective-permute-start.6 = (f32[3,128]{1,0:T(4,128)S(1)}, f32[3,128]{1,0:T(4,128)S(1)}, u32[]{:S(2)}, u32[]{:S(2)}) collective-permute-start(f32[3,128]{1,0:T(4,128)S(1)} %collective-permute-done), channel_id=1, source_target_pairs={{0,28},{4,0},{8,4},{12,8},{16,12},{20,16},{24,20},{28,24},{1,29},{... | collective-permute-start | bytes 4616 | tf_op jit(solution)/shard_map/ppermute | solution.py:32
  13.6 9.1 %collective-permute-start.9 = (f32[3,128]{1,0:T(4,128)S(1)}, f32[3,128]{1,0:T(4,128)}, u32[]{:S(2)}, u32[]{:S(2)}) collective-permute-start(f32[3,128]{1,0:T(4,128)S(1)} %collective-permute-done.3), channel_id=1, source_target_pairs={{0,4},{4,8},{8,12},{12,16},{16,20},{20,24},{24,28},{28,0},{1,5},{5... | collective-permute-start | bytes 4616 | tf_op jit(solution)/shard_map/ppermute | solution.py:32
  15.4 4.0 %collective-permute-start.11 = (s32[128]{0:T(128)S(1)}, s32[128]{0:T(128)S(1)}, u32[]{:S(2)}, u32[]{:S(2)}) collective-permute-start(s32[128]{0:T(128)S(1)} %collective-permute-done.5), channel_id=1, source_target_pairs={{0,4},{4,8},{8,12},{12,16},{16,20},{20,24},{24,28},{28,0},{1,5},{5... | collective-permute-start | bytes 1544 | tf_op jit(solution)/shard_map/ppermute | solution.py:32
  16.2 3.8 %collective-permute-start.8 = (s32[128]{0:T(128)S(1)}, s32[128]{0:T(128)S(1)}, u32[]{:S(2)}, u32[]{:S(2)}) collective-permute-start(s32[128]{0:T(128)S(1)} %collective-permute-done.2), channel_id=1, source_target_pairs={{0,28},{4,0},{8,4},{12,8},{16,12},{20,16},{24,20},{28,24},{1,29},{... | collective-permute-start | bytes 1544 | tf_op jit(solution)/shard_map/ppermute | solution.py:32
  19.5 3.8 %collective-permute-start.1 = (f32[16,128]{1,0:T(8,128)S(1)}, f32[16,128]{1,0:T(8,128)S(1)}, u32[]{:S(2)}, u32[]{:S(2)}) collective-permute-start(f32[16,128]{1,0:T(8,128)S(1)} %copy-done.6), channel_id=1, source_target_pairs={{0,28},{4,0},{8,4},{12,8},{16,12},{20,16},{24,20},{28,24},{1,29},{... | collective-permute-start | bytes 24584 | tf_op jit(solution)/shard_map/ppermute | solution.py:32
  20.0 9.0 %collective-permute-start.17 = (s32[128]{0:T(128)S(1)}, s32[128]{0:T(128)S(1)}, u32[]{:S(2)}, u32[]{:S(2)}) collective-permute-start(s32[128]{0:T(128)S(1)} %collective-permute-done.11), channel_id=1, source_target_pairs={{0,4},{4,8},{8,12},{12,16},{16,20},{20,24},{24,28},{28,0},{1,5},{5... | collective-permute-start | bytes 1544 | tf_op jit(solution)/shard_map/ppermute | solution.py:32
  20.5 12.4 %collective-permute-start.14 = (s32[128]{0:T(128)S(1)}, s32[128]{0:T(128)S(1)}, u32[]{:S(2)}, u32[]{:S(2)}) collective-permute-start(s32[128]{0:T(128)S(1)} %collective-permute-done.8), channel_id=1, source_target_pairs={{0,28},{4,0},{8,4},{12,8},{16,12},{20,16},{24,20},{28,24},{1,29},{... | collective-permute-start | bytes 1544 | tf_op jit(solution)/shard_map/ppermute | solution.py:32
  22.6 10.6 %collective-permute-start.12 = (f32[3,128]{1,0:T(4,128)S(1)}, f32[3,128]{1,0:T(4,128)S(1)}, u32[]{:S(2)}, u32[]{:S(2)}) collective-permute-start(f32[3,128]{1,0:T(4,128)S(1)} %collective-permute-done.6), channel_id=1, source_target_pairs={{0,28},{4,0},{8,4},{12,8},{16,12},{20,16},{24,20},{28,24},{1,29},{... | collective-permute-start | bytes 4616 | tf_op jit(solution)/shard_map/ppermute | solution.py:32
  22.7 18.7 %collective-permute-start.15 = (f32[3,128]{1,0:T(4,128)}, f32[3,128]{1,0:T(4,128)S(1)}, u32[]{:S(2)}, u32[]{:S(2)}) collective-permute-start(f32[3,128]{1,0:T(4,128)} %collective-permute-done.9), channel_id=1, source_target_pairs={{0,4},{4,8},{8,12},{12,16},{16,20},{20,24},{24,28},{28,0},{1,5},{5... | collective-permute-start | bytes 4616 | tf_op jit(solution)/shard_map/ppermute | solution.py:32
  23.3 4.0 %collective-permute-start.10 = (f32[16,128]{1,0:T(8,128)S(1)}, f32[16,128]{1,0:T(8,128)S(1)}, u32[]{:S(2)}, u32[]{:S(2)}) collective-permute-start(f32[16,128]{1,0:T(8,128)S(1)} %collective-permute-done.4), channel_id=1, source_target_pairs={{0,4},{4,8},{8,12},{12,16},{16,20},{20,24},{24,28},{28,0},{1,5},{5... | collective-permute-start | bytes 24584 | tf_op jit(solution)/shard_map/ppermute | solution.py:32
  27.3 1.4 %collective-permute-start.7 = (f32[16,128]{1,0:T(8,128)S(1)}, f32[16,128]{1,0:T(8,128)S(1)}, u32[]{:S(2)}, u32[]{:S(2)}) collective-permute-start(f32[16,128]{1,0:T(8,128)S(1)} %collective-permute-done.1), channel_id=1, source_target_pairs={{0,28},{4,0},{8,4},{12,8},{16,12},{20,16},{24,20},{28,24},{1,29},{... | collective-permute-start | bytes 24584 | tf_op jit(solution)/shard_map/ppermute | solution.py:32
  28.7 4.0 %collective-permute-start.16 = (f32[16,128]{1,0:T(8,128)S(1)}, f32[16,128]{1,0:T(8,128)S(1)}, u32[]{:S(2)}, u32[]{:S(2)}) collective-permute-start(f32[16,128]{1,0:T(8,128)S(1)} %collective-permute-done.10), channel_id=1, source_target_pairs={{0,4},{4,8},{8,12},{12,16},{16,20},{20,24},{24,28},{28,0},{1,5},{5... | collective-permute-start | bytes 24584 | tf_op jit(solution)/shard_map/ppermute | solution.py:32
  29.0 3.9 %collective-permute-start.13 = (f32[16,128]{1,0:T(8,128)S(1)}, f32[16,128]{1,0:T(8,128)S(1)}, u32[]{:S(2)}, u32[]{:S(2)}) collective-permute-start(f32[16,128]{1,0:T(8,128)S(1)} %collective-permute-done.7), channel_id=1, source_target_pairs={{0,28},{4,0},{8,4},{12,8},{16,12},{20,16},{24,20},{28,24},{1,29},{... | collective-permute-start | bytes 24584 | tf_op jit(solution)/shard_map/ppermute | solution.py:32
  52.6 2.2 %copy-start.2 = (f32[3,64,64]{2,1,0:T(8,128)S(1)}, f32[3,64,64]{2,1,0:T(8,128)}, u32[]{:S(2)}) copy-start(f32[3,64,64]{2,1,0:T(8,128)} %param.34) | copy-start | bytes 147460
  52.7 6.7 %collective-permute-start.18 = (f32[16,9,128]{2,0,1:T(8,128)S(1)}, f32[16,9,128]{2,0,1:T(8,128)S(1)}, u32[]{:S(2)}, u32[]{:S(2)}) collective-permute-start(f32[16,9,128]{2,0,1:T(8,128)S(1)} %add_multiply_fusion.6), channel_id=1, source_target_pairs={{0,1},{1,2},{2,3},{3,0},{4,5},{5,6},{6,7},{7,4},{8,9},{9,10},{10,1... | collective-permute-start | bytes 221192 | tf_op jit(solution)/shard_map/ppermute | solution.py:24
  59.3 6.4 %collective-permute-start.19 = (f32[16,9,128]{2,0,1:T(8,128)S(1)}, f32[16,9,128]{2,0,1:T(8,128)S(1)}, u32[]{:S(2)}, u32[]{:S(2)}) collective-permute-start(f32[16,9,128]{2,0,1:T(8,128)S(1)} %collective-permute-done.18), channel_id=1, source_target_pairs={{0,1},{1,2},{2,3},{3,0},{4,5},{5,6},{6,7},{7,4},{8,9},{9,10},{10,1... | collective-permute-start | bytes 221192 | tf_op jit(solution)/shard_map/ppermute | solution.py:24
  65.8 6.2 %collective-permute-start.20 = (f32[16,9,128]{2,0,1:T(8,128)S(1)}, f32[16,9,128]{2,0,1:T(8,128)S(1)}, u32[]{:S(2)}, u32[]{:S(2)}) collective-permute-start(f32[16,9,128]{2,0,1:T(8,128)S(1)} %collective-permute-done.19), channel_id=1, source_target_pairs={{0,1},{1,2},{2,3},{3,0},{4,5},{5,6},{6,7},{7,4},{8,9},{9,10},{10,1... | collective-permute-start | bytes 221192 | tf_op jit(solution)/shard_map/ppermute | solution.py:24
